TPU v7x, 512 devices: a whole 4x8x8 slice. The times are simulated.
512 devices in a mesh: row: 16 (over x, y_lo), blk: 32 (over y_hi, z, core).
Axes of the slice: x: 4, y: 8 (y_hi: 2, y_lo: 4; y = y_hi * 4 + y_lo), z: 8, core: 2. Of those that a mesh axis runs over, the one named last changes fastest.
Arguments:
- cells: bfloat16 [131072, 768], P(('row', 'blk')), may hold values from -12 to 12
- tile_rows: int32 [6144], P(('row', 'blk')), may hold values from 0 to 1, as said below
- tile_cols: int32 [6144], P(('row', 'blk')), may hold values from 0 to 5, as said below
- tile_count: int32 [512], P(('row', 'blk')), may hold values from 6 to 12, as said below
- halo_blocks: int32 [512], P(('row', 'blk')), may hold values from 0 to 1, as said below
- tile_vals: bfloat16 [6144, 128, 128], P(('row', 'blk')), may hold values from -0.375 to 0.375
- pool_ids: int32 [131072], P(('row', 'blk')), may hold values from 0 to 15, as said below
- w_msg: bfloat16 [768, 768], replicated, may hold values from -0.21875 to 0.21875
- w_query: bfloat16 [768, 768], replicated, may hold values from -1 to 2
- cotangent: bfloat16 [131072, 768], P(('row', 'blk')), may hold values from -6 to 6
Outputs:
- passed: bfloat16 [131072, 768], P(('row', 'blk'))
- attended: bfloat16 [131072, 768], P(('row', 'blk'))
- grad_cells: bfloat16 [131072, 768], P(('row', 'blk'))
Inputs may be any that keep to these rules, and one draw needn't show every extreme that they name: `tile_rows`: slot i of a partition's 12 slots, for i < 2, has row i. `tile_cols`: slot i of a partition, for i < 6, has column i; later slots have columns below 2. `tile_count`: slots of a partition at or beyond its count are unused. `halo_blocks`: distinct within one partition. `pool_ids`: every supernode of a partition has at least one of its cells; the first two cells of a partition lie in supernodes 0 and 1.
All inputs are finite; a program needn't handle non-finite values.
Results may differ from a plain program's by a relative error of at most 0.04.
The roundings to bfloat16 on the way count: a program that leaves them out, or rounds other values in their place, can miss the bound.
Values may be sent and summed in bfloat16 or wider, within the bound.
No kernel may reach another device: no remote copies, remote signals or barrier semaphores. Data moves between devices by JAX's collectives and lax.ppermute only.
A program may use at most 64 MiB of HBM per device.

v0:
```python
import jax
import jax.numpy as jnp
from jax import lax
from jax.sharding import PartitionSpec as P

D = 768
HEADS = 12
HEAD = 64
BLOCK = 128
NB = 2
HB = 1
SN_DEV = 16
EXT = 6
CELL_DEV = 256


def padded(value, sides, width):
    for axis, dim in sides:
        count, length = (lax.axis_size(axis), value.shape[dim])
        up = [(i, (i + 1) % count) for i in range(count - 1)]
        down = [(j, i) for i, j in up]
        last = lax.slice_in_dim(value, length - width, length, axis=dim)
        leading = lax.slice_in_dim(value, 0, width, axis=dim)
        before = lax.ppermute(last, axis, up)
        after = lax.ppermute(leading, axis, down)
        value = jnp.concatenate([before, value, after], axis=dim)
    return value


def passed_along(value, axis, steps):
    count = lax.axis_size(axis)
    leading, last = (max(0, -steps), min(count, count - steps))
    return lax.ppermute(value, axis, [(source, source + steps) for source in range(leading, last)])


def silu_slope(values):
    sigma = jax.nn.sigmoid(values)
    return sigma * (1.0 + values * (1.0 - sigma))


def body(
    cells,
    tile_rows,
    tile_cols,
    tile_count,
    halo_blocks,
    tile_vals,
    pool_ids,
    w_msg,
    w_query,
    cotangent,
):
    blocks = cells.reshape(NB, BLOCK, D)
    boundary = blocks[halo_blocks]
    beside_all = padded(boundary[None, None], (("row", 0), ("blk", 1)), 1)
    extended = jnp.concatenate(
        [blocks, beside_all[0, 1], beside_all[2, 1], beside_all[1, 0], beside_all[1, 2]], axis=0
    )
    live_count = tile_count[0]

    def add_tile(number, totals):
        picked = lax.dynamic_index_in_dim(extended, tile_cols[number], 0, keepdims=False)
        product = jnp.dot(tile_vals[number], picked, preferred_element_type=jnp.float32)
        return totals.at[tile_rows[number]].add(product)

    msg_sums = lax.fori_loop(0, live_count, add_tile, jnp.zeros((NB, BLOCK, D), jnp.float32))
    message = msg_sums.astype(jnp.bfloat16).reshape(CELL_DEV, D)
    hidden = jnp.dot(message, w_msg, preferred_element_type=jnp.float32)
    passed = (cells.astype(jnp.float32) + jax.nn.silu(hidden)).astype(jnp.bfloat16)
    member = pool_ids[None, :] == jnp.arange(SN_DEV, dtype=jnp.int32)[:, None]
    member_bf = member.astype(jnp.bfloat16)
    counts = jnp.sum(member.astype(jnp.float32), axis=1)
    root_count = jnp.sqrt(counts)[:, None]
    pooled = jnp.dot(member_bf, passed, preferred_element_type=jnp.float32)
    supern = (pooled / root_count).astype(jnp.bfloat16)
    query_proj = jnp.dot(passed, w_query, preferred_element_type=jnp.float32).astype(jnp.bfloat16)
    key_table = lax.all_gather(supern, "blk", axis=0, tiled=True)
    score_scale = HEAD ** (-0.5)
    queries = query_proj.reshape(CELL_DEV, HEADS, HEAD)
    key_rows = key_table.reshape(-1, HEADS, HEAD)
    grads = cotangent.reshape(CELL_DEV, HEADS, HEAD)
    scores = (
        jnp.einsum("qhe,khe->hqk", queries, key_rows, preferred_element_type=jnp.float32)
        * score_scale
    )
    weights = jnp.exp(scores - jnp.max(scores, axis=2, keepdims=True))
    weights = weights / jnp.sum(weights, axis=2, keepdims=True)
    rounded = weights.astype(jnp.bfloat16)
    values_sum = jnp.einsum("hqk,khe->qhe", rounded, key_rows, preferred_element_type=jnp.float32)
    centre = jnp.sum(grads.astype(jnp.float32) * values_sum, axis=2)
    slope = jnp.einsum("qhe,khe->hqk", grads, key_rows, preferred_element_type=jnp.float32)
    dscore = (weights * (slope - centre.T[:, :, None]) * score_scale).astype(jnp.bfloat16)
    dquery = (
        jnp.einsum("hqk,khe->qhe", dscore, key_rows, preferred_element_type=jnp.float32)
        .astype(jnp.bfloat16)
        .reshape(CELL_DEV, D)
    )
    from_scores = jnp.einsum("hqk,qhe->khe", dscore, queries, preferred_element_type=jnp.float32)
    from_values = jnp.einsum("hqk,qhe->khe", rounded, grads, preferred_element_type=jnp.float32)
    key_grad = lax.psum_scatter(
        (from_scores + from_values).reshape(lax.axis_size("blk") * SN_DEV, D),
        "blk",
        scatter_dimension=0,
        tiled=True,
    )
    pool_grad = (key_grad / root_count).astype(jnp.bfloat16)
    spread = jnp.einsum("sc,sf->cf", member_bf, pool_grad, preferred_element_type=jnp.float32)
    back_query = lax.dot_general(
        dquery, w_query, (((1,), (1,)), ((), ())), preferred_element_type=jnp.float32
    )
    through = (cotangent.astype(jnp.float32) + back_query + spread).astype(jnp.bfloat16)
    dhidden = (through.astype(jnp.float32) * silu_slope(hidden)).astype(jnp.bfloat16)
    dmessage = (
        lax.dot_general(
            dhidden, w_msg, (((1,), (1,)), ((), ())), preferred_element_type=jnp.float32
        )
        .astype(jnp.bfloat16)
        .reshape(NB, BLOCK, D)
    )

    def back_tile(number, totals):
        picked = lax.dynamic_index_in_dim(dmessage, tile_rows[number], 0, keepdims=False)
        product = lax.dot_general(
            tile_vals[number], picked, (((0,), (0,)), ((), ())), preferred_element_type=jnp.float32
        )
        return totals.at[tile_cols[number]].add(product)

    ext_grad = lax.fori_loop(0, live_count, back_tile, jnp.zeros((EXT, BLOCK, D), jnp.float32))
    returned = jnp.zeros((HB, BLOCK, D), jnp.float32)
    for offset, first_slot in ((1, NB + HB), (-1, NB)):
        returned = returned + passed_along(ext_grad[first_slot : first_slot + HB], "row", offset)
    for offset, first_slot in ((1, NB + 3 * HB), (-1, NB + 2 * HB)):
        returned = returned + passed_along(ext_grad[first_slot : first_slot + HB], "blk", offset)
    summed = through.astype(jnp.float32).reshape(NB, BLOCK, D) + ext_grad[:NB]
    summed = summed.at[halo_blocks].add(returned)
    attended = values_sum.astype(jnp.bfloat16).reshape(CELL_DEV, D)
    return (passed, attended, summed.astype(jnp.bfloat16).reshape(CELL_DEV, D))


def solution(mesh):
    return jax.shard_map(
        body,
        mesh=mesh,
        in_specs=(
            P(("row", "blk"), None),
            P(("row", "blk")),
            P(("row", "blk")),
            P(("row", "blk")),
            P(("row", "blk")),
            P(("row", "blk"), None, None),
            P(("row", "blk")),
            P(),
            P(),
            P(("row", "blk"), None),
        ),
        out_specs=(P(("row", "blk"), None), P(("row", "blk"), None), P(("row", "blk"), None)),
        check_vma=False,
    )
```

profile of v0, /device:TPU:1, one launch (start us, length us, event | category | flops | bytes accessed | tf_op | source)
XLA Modules:
  0.0 499.1 jit_solution(8271028985176664791)
XLA Ops:
  9.0 4.0 collective-permute-start
  16.5 8.1 %collective-permute-done.1 = bf16[1,1,1,128,768]{4,3,2,1,0:T(8,128)(2,1)S(1)} collective-permute-done((bf16[1,1,1,128,768]{4,3,2,1,0:T(8,128)(2,1)S(1)}, bf16[1,1,1,128,768]{4,3,2,1,0:T(8,128)(2,1)S(1)}, u32[]{:S(2)}, u32[]{:S(2)}) %collective-permute-start.1) | collective-permute-done | bytes 196640 | tf_op jit(solution)/shard_map/ppermute | solution.py:25
  24.6 5.3 %collective-permute-start.2 = (bf16[3,1,1,128,768]{4,3,2,1,0:T(8,128)(2,1)S(1)}, bf16[3,1,1,128,768]{4,3,2,1,0:T(8,128)(2,1)S(1)}, u32[]{:S(2)}, u32[]{:S(2)}) collective-permute-start(bf16[3,1,1,128,768]{4,3,2,1,0:T(8,128)(2,1)S(1)} %pad_maximum_fusion), channel_id=1, source_target_pairs={{0,1},{1,2},{2,3},{3,4},{4,5},{5,6},{6,7},{7,8},{8,9},{9,10},{10,1... | collective-permute-start | bytes 1769480 | tf_op jit(solution)/shard_map/ppermute | solution.py:24
  29.9 1.9 collective-permute-start.3
  31.9 4.8 collective-permute-done.2
  36.7 4.4 collective-permute-done.3
  41.2 48.9 %while.24 = (s32[]{:T(128)}, f32[2,128,768]{2,1,0:T(8,128)S(1)}, s32[]{:T(128)}, s32[12]{0:T(128)S(1)}, bf16[12,128,128]{2,1,0:T(8,128)(2,1)}, /*index=5*/s32[12...) while((s32[]{:T(128)}, f32[2,128,768]{2,1,0:T(8,128)S(1)}, ...), condition=%wide.region_2.3_spmd, body=%wide.region_0.2_spmd.sunk | while | flops 25362460 | bytes 1017128 | solution.py:66
  90.3 2.4 add_convert_fusion
  93.4 105.0 %all_gather.3 = bf16[512,768]{1,0:T(8,128)(2,1)} all-gather(bf16[16,768]{1,0:T(8,128)(2,1)S(1)} %fusion.26), channel_id=1, replica_groups=mesh['row'=16,'blk'=32] {'blk'}, dimensions={0}, use_global_device_ids=true | all-gather | bytes 811008 | tf_op jit(solution)/shard_map/all_gather | solution.py:77
  199.8 2.2 convolution_convert_fusion.2
  203.2 4.6 fusion.39
  207.9 3.3 fusion.23
  218.7 3.1 convolution_convert_fusion.1
  223.2 123.1 %reduce-scatter.2.cloned.1.call-done = f32[16,768]{1,0:T(8,128)} async-done(((f32[512,768]{1,0:T(8,128)}), f32[16,768]{1,0:T(8,128)}) %reduce-scatter.2.cloned.1.call-update) | async-done | bytes 49168 | tf_op jit(solution)/shard_map/reduce_scatter | solution.py:100
  347.9 2.8 convolution_convert_fusion
  351.4 53.5 %while.25 = (s32[]{:T(128)}, f32[6,128,768]{2,1,0:T(8,128)S(1)}, s32[]{:T(128)}, s32[12]{0:T(128)S(1)}, bf16[12,128,128]{2,1,0:T(8,128)(2,1)}, /*index=5*/s32[12...) while((s32[]{:T(128)}, f32[6,128,768]{2,1,0:T(8,128)S(1)}, ...), condition=%wide.region_10.11_spmd, body=%wide.region_8.10_spmd.sunk | while | flops 25362460 | bytes 1017128 | solution.py:128
  367.1 1.9 fusion.74
  406.0 60.6 %collective-permute-start.7 = (f32[1,128,768]{2,1,0:T(8,128)}, f32[1,128,768]{2,1,0:T(8,128)}, u32[]{:S(2)}, u32[]{:S(2)}) collective-permute-start(f32[1,128,768]{2,1,0:T(8,128)} %get-tuple-element.166), channel_id=1, source_target_pairs={{1,0},{2,1},{3,2},{4,3},{5,4},{6,5},{7,6},{8,7},{9,8},{10,9},{11,1... | collective-permute-start | bytes 1179656 | tf_op jit(solution)/shard_map/ppermute | solution.py:33
  466.6 1.9 collective-permute-start.6
  468.5 3.6 collective-permute-start.4
  474.2 1.9 copy.34
  477.3 3.2 collective-permute-done.4
  480.5 8.7 %collective-permute-done.5 = f32[1,128,768]{2,1,0:T(8,128)} collective-permute-done((f32[1,128,768]{2,1,0:T(8,128)}, f32[1,128,768]{2,1,0:T(8,128)}, u32[]{:S(2)}, u32[]{:S(2)}) %collective-permute-start.5) | collective-permute-done | bytes 393248 | tf_op jit(solution)/shard_map/ppermute | solution.py:33
  489.3 2.2 fusion.29
  (115 shorter events, 67.6 us)
Async XLA Ops:
  7.2 83.1 %copy-start = (bf16[768,768]{1,0:T(8,128)(2,1)S(1)}, bf16[768,768]{1,0:T(8,128)(2,1)}, u32[]{:S(2)}) copy-start(bf16[768,768]{1,0:T(8,128)(2,1)} %param.27) | copy-start | bytes 3538948
  7.2 22.7 %copy-start.10 = (bf16[256,768]{1,0:T(8,128)(2,1)S(1)}, bf16[256,768]{1,0:T(8,128)(2,1)}, u32[]{:S(2)}) copy-start(bf16[256,768]{1,0:T(8,128)(2,1)} %param.20) | copy-start | bytes 1179652
  7.2 339.2 %reduce-scatter.2.cloned.1.call-start = ((), (), s32[]{:S(2)}) async-start(), calls=%async_computation.1 | async-start | bytes 1622016 | tf_op jit(solution)/shard_map/reduce_scatter | solution.py:100
  9.0 7.5 %collective-permute-start = (bf16[1,1,1,128,768]{4,3,2,1,0:T(8,128)(2,1)S(1)}, bf16[1,1,1,128,768]{4,3,2,1,0:T(8,128)(2,1)S(1)}, u32[]{:S(2)}, u32[]{:S(2)}) collective-permute-start(bf16[1,1,1,128,768]{4,3,2,1,0:T(8,128)(2,1)S(1)} %dynamic-slice_bitcast_fusion), channel_id=1, source_target_pairs={{0,32},{32,64},{64,96},{96,128},{128,160},{160,192},{192,224},{224... | collective-permute-start | bytes 589832 | tf_op jit(solution)/shard_map/ppermute | solution.py:24
  13.0 11.5 %collective-permute-start.1 = (bf16[1,1,1,128,768]{4,3,2,1,0:T(8,128)(2,1)S(1)}, bf16[1,1,1,128,768]{4,3,2,1,0:T(8,128)(2,1)S(1)}, u32[]{:S(2)}, u32[]{:S(2)}) collective-permute-start(bf16[1,1,1,128,768]{4,3,2,1,0:T(8,128)(2,1)S(1)} %dynamic-slice_bitcast_fusion), channel_id=1, source_target_pairs={{32,0},{64,32},{96,64},{128,96},{160,128},{192,160},{224,192},{256... | collective-permute-start | bytes 589832 | tf_op jit(solution)/shard_map/ppermute | solution.py:25
  15.5 197.6 %copy-start.5 = (bf16[256,768]{0,1:T(8,128)(2,1)}, bf16[256,768]{0,1:T(8,128)(2,1)S(1)}, u32[]{:S(2)}) copy-start(bf16[256,768]{0,1:T(8,128)(2,1)S(1)} %copy.31) | copy-start | bytes 1179652
  15.5 25.7 %copy-start.11 = (s32[3]{0:T(128)S(1)}, s32[3]{0:T(128)}, u32[]{:S(2)}) copy-start(s32[3]{0:T(128)} %constant.110.clone.1) | copy-start | bytes 40
  15.5 25.7 %copy-start.14 = (s32[12]{0:T(128)S(1)}, s32[12]{0:T(128)}, u32[]{:S(2)}) copy-start(s32[12]{0:T(128)} %param.21) | copy-start | bytes 148
  15.5 25.7 %copy-start.15 = (s32[12]{0:T(128)S(1)}, s32[12]{0:T(128)}, u32[]{:S(2)}) copy-start(s32[12]{0:T(128)} %param.22) | copy-start | bytes 148
  24.6 12.1 %collective-permute-start.2 = (bf16[3,1,1,128,768]{4,3,2,1,0:T(8,128)(2,1)S(1)}, bf16[3,1,1,128,768]{4,3,2,1,0:T(8,128)(2,1)S(1)}, u32[]{:S(2)}, u32[]{:S(2)}) collective-permute-start(bf16[3,1,1,128,768]{4,3,2,1,0:T(8,128)(2,1)S(1)} %pad_maximum_fusion), channel_id=1, source_target_pairs={{0,1},{1,2},{2,3},{3,4},{4,5},{5,6},{6,7},{7,8},{8,9},{9,10},{10,1... | collective-permute-start | bytes 1769480 | tf_op jit(solution)/shard_map/ppermute | solution.py:24
  29.9 11.2 %collective-permute-start.3 = (bf16[3,1,1,128,768]{4,3,2,1,0:T(8,128)(2,1)S(1)}, bf16[3,1,1,128,768]{4,3,2,1,0:T(8,128)(2,1)S(1)}, u32[]{:S(2)}, u32[]{:S(2)}) collective-permute-start(bf16[3,1,1,128,768]{4,3,2,1,0:T(8,128)(2,1)S(1)} %pad_maximum_fusion), channel_id=1, source_target_pairs={{1,0},{2,1},{3,2},{4,3},{5,4},{6,5},{7,6},{8,7},{9,8},{10,9},{11,1... | collective-permute-start | bytes 1769480 | tf_op jit(solution)/shard_map/ppermute | solution.py:25
  90.3 2.4 copy-start.13
  92.7 0.7 copy-start.9
  92.7 107.2 %copy-start.3 = (bf16[768,768]{1,0:T(8,128)(2,1)S(1)}, bf16[768,768]{1,0:T(8,128)(2,1)}, u32[]{:S(2)}) copy-start(bf16[768,768]{1,0:T(8,128)(2,1)} %param.28) | copy-start | bytes 3538948
  207.9 5.2 %copy-start.2 = (f32[12,256,512]{2,1,0:T(8,128)S(1)}, f32[12,256,512]{2,1,0:T(8,128)}, u32[]{:S(2)}) copy-start(f32[12,256,512]{2,1,0:T(8,128)} %get-tuple-element.174) | copy-start | bytes 18874372
  214.7 1.6 copy-start.1
  214.8 1.6 copy-start.6
  218.7 3.1 copy-start.4
  218.7 3.1 copy-start.8
  347.9 2.8 copy-start.7
  406.0 71.3 %collective-permute-start.7 = (f32[1,128,768]{2,1,0:T(8,128)}, f32[1,128,768]{2,1,0:T(8,128)}, u32[]{:S(2)}, u32[]{:S(2)}) collective-permute-start(f32[1,128,768]{2,1,0:T(8,128)} %get-tuple-element.166), channel_id=1, source_target_pairs={{1,0},{2,1},{3,2},{4,3},{5,4},{6,5},{7,6},{8,7},{9,8},{10,9},{11,1... | collective-permute-start | bytes 1179656 | tf_op jit(solution)/shard_map/ppermute | solution.py:33
  466.6 10.7 %collective-permute-start.6 = (f32[1,128,768]{2,1,0:T(8,128)}, f32[1,128,768]{2,1,0:T(8,128)}, u32[]{:S(2)}, u32[]{:S(2)}) collective-permute-start(f32[1,128,768]{2,1,0:T(8,128)} %get-tuple-element.167), channel_id=1, source_target_pairs={{0,1},{1,2},{2,3},{3,4},{4,5},{5,6},{6,7},{7,8},{8,9},{9,10},{10,1... | collective-permute-start | bytes 1179656 | tf_op jit(solution)/shard_map/ppermute | solution.py:33
  468.5 12.0 %collective-permute-start.4 = (f32[1,128,768]{2,1,0:T(8,128)}, f32[1,128,768]{2,1,0:T(8,128)}, u32[]{:S(2)}, u32[]{:S(2)}) collective-permute-start(f32[1,128,768]{2,1,0:T(8,128)} %get-tuple-element.168), channel_id=1, source_target_pairs={{0,32},{32,64},{64,96},{96,128},{128,160},{160,192},{192,224},{224... | collective-permute-start | bytes 1179656 | tf_op jit(solution)/shard_map/ppermute | solution.py:33
  472.1 17.2 %collective-permute-start.5 = (f32[1,128,768]{2,1,0:T(8,128)}, f32[1,128,768]{2,1,0:T(8,128)}, u32[]{:S(2)}, u32[]{:S(2)}) collective-permute-start(f32[1,128,768]{2,1,0:T(8,128)} %get-tuple-element.165), channel_id=1, source_target_pairs={{32,0},{64,32},{96,64},{128,96},{160,128},{192,160},{224,192},{256... | collective-permute-start | bytes 1179656 | tf_op jit(solution)/shard_map/ppermute | solution.py:33
  (2 other events, 1.3 us)
Sparse Core Ops, SparseCore 0:
  218.8 127.5 reduce-scatter.1
where the time goes:
time: 503 us; the launch traced here: 499 us
  waiting for transfers between devices  152 us (30%)
  blocking collectives  105 us (21%)
  starting transfers between devices  79.9 us (16%)
  loops' own time  57.3 us (11%)
  matrix products  43.9 us (9%)
  local copies, waits for them, and re-layouts  27 us (5%)
  other arithmetic  18.4 us (4%)
  between operations  15.2 us (3%)
    reduce_scatter x1, waiting for transfers between devices, body(): lax.psum_scatter((from_scores + from_values).reshape(lax.axis_size('blk')...  123 us
    all_gather x1, blocking collectives, body(): key_table = lax.all_gather(supern, 'blk', axis=0, tiled=True)  105 us
    ppermute x4, starting transfers between devices, passed_along(): lax.ppermute(value, axis, [(source, source + steps) for source in range(l...  67.4 us
    another operation x1, loops' own time, body(): lax.fori_loop(0, live_count, back_tile, jnp.zeros((EXT, BLOCK, D), jnp.fl...  29.5 us
    another operation x1, loops' own time, body(): lax.fori_loop(0, live_count, add_tile, jnp.zeros((NB, BLOCK, D), jnp.floa...  27.8 us
    ppermute x2, waiting for transfers between devices, padded(): after = lax.ppermute(leading, axis, down)  12.5 us
    ppermute x4, waiting for transfers between devices, passed_along(): lax.ppermute(value, axis, [(source, source + steps) for source in range(l...  12 us
    dot_general x6, matrix products, back_tile(): lax.dot_general(tile_vals[number], picked, (((0,), (0,)), ((), ())), pref...  11.3 us
  transfers between devices with their start and end apart: 9, of which 6 were waited for; matrix products, arithmetic and copies ran while one was open for 2% of the time, Pallas kernels for 0%

commit v1 on v0

--- a/solution.py
+++ b/solution.py
@@ -1,7 +1,9 @@
+import functools
 import jax
 import jax.numpy as jnp
 from jax import lax
 from jax.sharding import PartitionSpec as P
+from jax.lax import all_to_all, psum
 
 D = 768
 HEADS = 12
@@ -12,6 +14,16 @@
 SN_DEV = 16
 EXT = 6
 CELL_DEV = 256
+
+
+def close_tasks_here(my_data, d0):
+    return jnp.concatenate(
+        all_to_all(jnp.stack([my_data for _ in range(psum(1, "blk"))], axis=0), "blk", 0, 0),
+        axis=d0,
+    )
+
+
+edge_supply = functools.partial(close_tasks_here, d0=0)
 
 
 def padded(value, sides, width):
@@ -74,7 +86,7 @@
     pooled = jnp.dot(member_bf, passed, preferred_element_type=jnp.float32)
     supern = (pooled / root_count).astype(jnp.bfloat16)
     query_proj = jnp.dot(passed, w_query, preferred_element_type=jnp.float32).astype(jnp.bfloat16)
-    key_table = lax.all_gather(supern, "blk", axis=0, tiled=True)
+    key_table = edge_supply(supern)
     score_scale = HEAD ** (-0.5)
     queries = query_proj.reshape(CELL_DEV, HEADS, HEAD)
     key_rows = key_table.reshape(-1, HEADS, HEAD)

time: 503 us -> 473 us (0.940)
  blocking collectives: 105 us -> 0 us
  starting transfers between devices: 79.9 us -> 137 us
  waiting for transfers between devices: 152 us -> 175 us
    all_gather x1 -> x0, blocking collectives: 105 us -> none  [body(): key_table = lax.all_gather(supern, 'blk', axis=0, tiled=True)]
    all_to_all x0 -> x1, starting transfers between devices: none -> 63.2 us  [close_tasks_here(): all_to_all(jnp.stack([my_data for _ in range(psum(1, 'blk'))], axis=0), '...]
    all_to_all x0 -> x1, waiting for transfers between devices: none -> 18.8 us  [close_tasks_here(): all_to_all(jnp.stack([my_data for _ in range(psum(1, 'blk'))], axis=0), '...]
    another operation x0 -> x3, local copies, waits for them, and re-layouts: none -> 5.93 us  [the longest x2 4.93 us: body(): key_rows = key_table.reshape(-1, HEADS, HEAD)]
    ppermute x4, starting transfers between devices: 67.4 us -> 61.5 us  [passed_along(): lax.ppermute(value, axis, [(source, source + steps) for source in range(l...]
  transfers between devices with their start and end apart: 9 -> 10, of which waited for: 6 -> 8; matrix products, arithmetic and copies ran while one was open for 2% -> 2% of each run, Pallas kernels for 0% -> 0%
where the time goes in v1:
time: 473 us; the launch traced here: 469 us
  waiting for transfers between devices  175 us (37%)
  starting transfers between devices  137 us (29%)
  loops' own time  53.6 us (11%)
  matrix products  40.5 us (9%)
  local copies, waits for them, and re-layouts  30.5 us (6%)
  other arithmetic  17.5 us (4%)
  between operations  15.2 us (3%)
    reduce_scatter x1, waiting for transfers between devices, body(): lax.psum_scatter((from_scores + from_values).reshape(lax.axis_size('blk')...  125 us
    all_to_all x1, starting transfers between devices, close_tasks_here(): all_to_all(jnp.stack([my_data for _ in range(psum(1, 'blk'))], axis=0), '...  63.2 us
    ppermute x4, starting transfers between devices, passed_along(): lax.ppermute(value, axis, [(source, source + steps) for source in range(l...  61.5 us
    another operation x1, loops' own time, body(): lax.fori_loop(0, live_count, add_tile, jnp.zeros((NB, BLOCK, D), jnp.floa...  28.1 us
    another operation x1, loops' own time, body(): lax.fori_loop(0, live_count, back_tile, jnp.zeros((EXT, BLOCK, D), jnp.fl...  25.5 us
    all_to_all x1, waiting for transfers between devices, close_tasks_here(): all_to_all(jnp.stack([my_data for _ in range(psum(1, 'blk'))], axis=0), '...  18.8 us
    ppermute x2, waiting for transfers between devices, padded(): after = lax.ppermute(leading, axis, down)  14.4 us
    ppermute x4, waiting for transfers between devices, passed_along(): lax.ppermute(value, axis, [(source, source + steps) for source in range(l...  12 us
  transfers between devices with their start and end apart: 10, of which 8 were waited for; matrix products, arithmetic and copies ran while one was open for 2% of the time, Pallas kernels for 0%

profile of v1, /device:TPU:1, one launch (start us, length us, event | category | flops | bytes accessed | tf_op | source)
XLA Modules:
  0.0 469.2 jit_solution(1364602197057019336)
XLA Ops:
  8.9 4.0 collective-permute-start
  15.5 8.9 %collective-permute-done.1 = bf16[1,1,1,128,768]{4,3,2,1,0:T(8,128)(2,1)S(1)} collective-permute-done((bf16[1,1,1,128,768]{4,3,2,1,0:T(8,128)(2,1)S(1)}, bf16[1,1,1,128,768]{4,3,2,1,0:T(8,128)(2,1)S(1)}, u32[]{:S(2)}, u32[]{:S(2)}) %collective-permute-start.1) | collective-permute-done | bytes 196640 | tf_op jit(solution)/shard_map/ppermute | solution.py:37
  24.6 5.3 %collective-permute-start.2 = (bf16[3,1,1,128,768]{4,3,2,1,0:T(8,128)(2,1)S(1)}, bf16[3,1,1,128,768]{4,3,2,1,0:T(8,128)(2,1)S(1)}, u32[]{:S(2)}, u32[]{:S(2)}) collective-permute-start(bf16[3,1,1,128,768]{4,3,2,1,0:T(8,128)(2,1)S(1)} %pad_maximum_fusion), channel_id=1, source_target_pairs={{0,1},{1,2},{2,3},{3,4},{4,5},{5,6},{6,7},{7,8},{8,9},{9,10},{10,1... | collective-permute-start | bytes 1769480 | tf_op jit(solution)/shard_map/ppermute | solution.py:36
  30.9 1.9 collective-permute-start.3
  32.9 3.8 collective-permute-done.2
  36.7 5.4 %collective-permute-done.3 = bf16[3,1,1,128,768]{4,3,2,1,0:T(8,128)(2,1)S(1)} collective-permute-done((bf16[3,1,1,128,768]{4,3,2,1,0:T(8,128)(2,1)S(1)}, bf16[3,1,1,128,768]{4,3,2,1,0:T(8,128)(2,1)S(1)}, u32[]{:S(2)}, u32[]{:S(2)}) %collective-permute-start.3) | collective-permute-done | bytes 589856 | tf_op jit(solution)/shard_map/ppermute | solution.py:37
  42.2 49.0 %while.24 = (s32[]{:T(128)}, f32[2,128,768]{2,1,0:T(8,128)S(1)}, s32[]{:T(128)}, s32[12]{0:T(128)S(1)}, bf16[12,128,128]{2,1,0:T(8,128)(2,1)}, /*index=5*/s32[12...) while((s32[]{:T(128)}, f32[2,128,768]{2,1,0:T(8,128)S(1)}, ...), condition=%wide.region_2.3_spmd, body=%wide.region_0.2_spmd.sunk | while | flops 25362460 | bytes 1017128 | solution.py:78
  93.9 63.2 %all-to-all-start = ((bf16[32,16,768]{2,1,0:T(8,128)(2,1)}), bf16[32,16,768]{2,1,0:T(8,128)(2,1)}, u32[]{:S(2)}, u32[]{:S(2)}) async-start(bf16[32,16,768]{2,1,0:T(8,128)(2,1)} %stack.2), calls=%async_computation | async-start | bytes 1572864 | tf_op jit(solution)/shard_map/all_to_all | solution.py:21
  159.4 18.8 %all-to-all-done = bf16[32,16,768]{2,1,0:T(8,128)(2,1)} async-done(((bf16[32,16,768]{2,1,0:T(8,128)(2,1)}), bf16[32,16,768]{2,1,0:T(8,128)(2,1)}, u32[]{:S(2)}, u32[]{:S(2)}) %all-to-all-start) | async-done | bytes 786464 | tf_op jit(solution)/shard_map/all_to_all | solution.py:21
  178.3 2.7 reshape_reshape.3
  181.0 2.2 copy.31
  183.2 5.9 %fusion.39 = (f32[12,256]{1,0:T(8,128)S(1)}, f32[12,256,512]{2,1,0:T(8,128)}) fusion(bf16[256,12,64]{0,2,1:T(8,128)(2,1)} %bitcast.128, bf16[512,12,64]{0,2,1:T(8,128)(2,1)} %copy.31), kind=kOutput, calls=%fused_computation.69 | convolution fusion | flops 206045696 | bytes 7483392 | tf_op jit(solution)/shard_map/sub | solution.py:98
  189.1 3.3 fusion.23
  199.9 3.1 convolution_convert_fusion.1
  203.5 125.2 %reduce-scatter.2.cloned.1.call-done = f32[16,768]{1,0:T(8,128)} async-done(((f32[512,768]{1,0:T(8,128)}), f32[16,768]{1,0:T(8,128)}) %reduce-scatter.2.cloned.1.call-update) | async-done | bytes 49168 | tf_op jit(solution)/shard_map/reduce_scatter | solution.py:112
  329.9 2.8 convolution_convert_fusion
  333.4 47.5 %while.25 = (s32[]{:T(128)}, f32[6,128,768]{2,1,0:T(8,128)S(1)}, s32[]{:T(128)}, s32[12]{0:T(128)S(1)}, bf16[12,128,128]{2,1,0:T(8,128)(2,1)}, /*index=5*/s32[12...) while((s32[]{:T(128)}, f32[6,128,768]{2,1,0:T(8,128)S(1)}, ...), condition=%wide.region_10.11_spmd, body=%wide.region_8.10_spmd.sunk | while | flops 25362460 | bytes 1017128 | solution.py:140
  382.1 54.7 %collective-permute-start.7 = (f32[1,128,768]{2,1,0:T(8,128)}, f32[1,128,768]{2,1,0:T(8,128)}, u32[]{:S(2)}, u32[]{:S(2)}) collective-permute-start(f32[1,128,768]{2,1,0:T(8,128)} %get-tuple-element.166), channel_id=1, source_target_pairs={{1,0},{2,1},{3,2},{4,3},{5,4},{6,5},{7,6},{8,7},{9,8},{10,9},{11,1... | collective-permute-start | bytes 1179656 | tf_op jit(solution)/shard_map/ppermute | solution.py:45
  436.8 1.9 collective-permute-start.6
  438.7 3.6 collective-permute-start.4
  444.4 1.9 copy.37
  447.5 3.2 collective-permute-done.4
  450.7 8.8 %collective-permute-done.5 = f32[1,128,768]{2,1,0:T(8,128)} collective-permute-done((f32[1,128,768]{2,1,0:T(8,128)}, f32[1,128,768]{2,1,0:T(8,128)}, u32[]{:S(2)}, u32[]{:S(2)}) %collective-permute-start.5) | collective-permute-done | bytes 393248 | tf_op jit(solution)/shard_map/ppermute | solution.py:45
  459.5 2.0 fusion.29
  (122 shorter events, 67.7 us)
Async XLA Ops:
  7.2 84.1 %copy-start = (bf16[768,768]{1,0:T(8,128)(2,1)S(1)}, bf16[768,768]{1,0:T(8,128)(2,1)}, u32[]{:S(2)}) copy-start(bf16[768,768]{1,0:T(8,128)(2,1)} %param.27) | copy-start | bytes 3538948
  7.9 34.2 %copy-start.13 = (s32[3]{0:T(128)S(1)}, s32[3]{0:T(128)}, u32[]{:S(2)}) copy-start(s32[3]{0:T(128)} %constant.110.clone.1) | copy-start | bytes 40
  7.9 34.2 %copy-start.16 = (s32[12]{0:T(128)S(1)}, s32[12]{0:T(128)}, u32[]{:S(2)}) copy-start(s32[12]{0:T(128)} %param.21) | copy-start | bytes 148
  7.9 34.2 %copy-start.17 = (s32[12]{0:T(128)S(1)}, s32[12]{0:T(128)}, u32[]{:S(2)}) copy-start(s32[12]{0:T(128)} %param.22) | copy-start | bytes 148
  8.9 6.6 %collective-permute-start = (bf16[1,1,1,128,768]{4,3,2,1,0:T(8,128)(2,1)S(1)}, bf16[1,1,1,128,768]{4,3,2,1,0:T(8,128)(2,1)S(1)}, u32[]{:S(2)}, u32[]{:S(2)}) collective-permute-start(bf16[1,1,1,128,768]{4,3,2,1,0:T(8,128)(2,1)S(1)} %dynamic-slice_bitcast_fusion), channel_id=1, source_target_pairs={{0,32},{32,64},{64,96},{96,128},{128,160},{160,192},{192,224},{224... | collective-permute-start | bytes 589832 | tf_op jit(solution)/shard_map/ppermute | solution.py:36
  13.0 11.5 %collective-permute-start.1 = (bf16[1,1,1,128,768]{4,3,2,1,0:T(8,128)(2,1)S(1)}, bf16[1,1,1,128,768]{4,3,2,1,0:T(8,128)(2,1)S(1)}, u32[]{:S(2)}, u32[]{:S(2)}) collective-permute-start(bf16[1,1,1,128,768]{4,3,2,1,0:T(8,128)(2,1)S(1)} %dynamic-slice_bitcast_fusion), channel_id=1, source_target_pairs={{32,0},{64,32},{96,64},{128,96},{160,128},{192,160},{224,192},{256... | collective-permute-start | bytes 589832 | tf_op jit(solution)/shard_map/ppermute | solution.py:37
  24.6 12.1 %collective-permute-start.2 = (bf16[3,1,1,128,768]{4,3,2,1,0:T(8,128)(2,1)S(1)}, bf16[3,1,1,128,768]{4,3,2,1,0:T(8,128)(2,1)S(1)}, u32[]{:S(2)}, u32[]{:S(2)}) collective-permute-start(bf16[3,1,1,128,768]{4,3,2,1,0:T(8,128)(2,1)S(1)} %pad_maximum_fusion), channel_id=1, source_target_pairs={{0,1},{1,2},{2,3},{3,4},{4,5},{5,6},{6,7},{7,8},{8,9},{9,10},{10,1... | collective-permute-start | bytes 1769480 | tf_op jit(solution)/shard_map/ppermute | solution.py:36
  30.9 11.2 %collective-permute-start.3 = (bf16[3,1,1,128,768]{4,3,2,1,0:T(8,128)(2,1)S(1)}, bf16[3,1,1,128,768]{4,3,2,1,0:T(8,128)(2,1)S(1)}, u32[]{:S(2)}, u32[]{:S(2)}) collective-permute-start(bf16[3,1,1,128,768]{4,3,2,1,0:T(8,128)(2,1)S(1)} %pad_maximum_fusion), channel_id=1, source_target_pairs={{1,0},{2,1},{3,2},{4,3},{5,4},{6,5},{7,6},{8,7},{9,8},{10,9},{11,1... | collective-permute-start | bytes 1769480 | tf_op jit(solution)/shard_map/ppermute | solution.py:37
  42.2 49.1 %copy-start.12 = (bf16[256,768]{1,0:T(8,128)(2,1)S(1)}, bf16[256,768]{1,0:T(8,128)(2,1)}, u32[]{:S(2)}) copy-start(bf16[256,768]{1,0:T(8,128)(2,1)} %param.20) | copy-start | bytes 1179652
  92.7 65.8 %copy-start.11 = (bf16[256,768]{1,0:T(8,128)(2,1)}, bf16[256,768]{1,0:T(8,128)(2,1)S(1)}, u32[]{:S(2)}) copy-start(bf16[256,768]{1,0:T(8,128)(2,1)S(1)} %get-tuple-element.171) | copy-start | bytes 1179652
  92.7 64.4 %copy-start.9 = (bf16[256,768]{1,0:T(8,128)(2,1)S(1)}, bf16[256,768]{1,0:T(8,128)(2,1)}, u32[]{:S(2)}) copy-start(bf16[256,768]{1,0:T(8,128)(2,1)} %param.29) | copy-start | bytes 1179652
  92.7 65.3 %copy-start.4 = (bf16[768,768]{1,0:T(8,128)(2,1)S(1)}, bf16[768,768]{1,0:T(8,128)(2,1)}, u32[]{:S(2)}) copy-start(bf16[768,768]{1,0:T(8,128)(2,1)} %param.28) | copy-start | bytes 3538948
  93.9 84.4 %all-to-all-start = ((bf16[32,16,768]{2,1,0:T(8,128)(2,1)}), bf16[32,16,768]{2,1,0:T(8,128)(2,1)}, u32[]{:S(2)}, u32[]{:S(2)}) async-start(bf16[32,16,768]{2,1,0:T(8,128)(2,1)} %stack.2), calls=%async_computation | async-start | bytes 1572864 | tf_op jit(solution)/shard_map/all_to_all | solution.py:21
  157.0 171.8 %reduce-scatter.2.cloned.1.call-start = ((), (), s32[]{:S(2)}) async-start(), calls=%async_computation.2 | async-start | bytes 1622016 | tf_op jit(solution)/shard_map/reduce_scatter | solution.py:112
  189.1 3.3 copy-start.2
  189.1 3.3 copy-start.6
  189.1 5.2 %copy-start.3 = (f32[12,256,512]{2,1,0:T(8,128)S(1)}, f32[12,256,512]{2,1,0:T(8,128)}, u32[]{:S(2)}) copy-start(f32[12,256,512]{2,1,0:T(8,128)} %get-tuple-element.174) | copy-start | bytes 18874372
  199.9 3.1 copy-start.5
  199.9 3.1 copy-start.10
  329.9 2.8 copy-start.7
  382.1 65.4 %collective-permute-start.7 = (f32[1,128,768]{2,1,0:T(8,128)}, f32[1,128,768]{2,1,0:T(8,128)}, u32[]{:S(2)}, u32[]{:S(2)}) collective-permute-start(f32[1,128,768]{2,1,0:T(8,128)} %get-tuple-element.166), channel_id=1, source_target_pairs={{1,0},{2,1},{3,2},{4,3},{5,4},{6,5},{7,6},{8,7},{9,8},{10,9},{11,1... | collective-permute-start | bytes 1179656 | tf_op jit(solution)/shard_map/ppermute | solution.py:45
  436.8 10.7 %collective-permute-start.6 = (f32[1,128,768]{2,1,0:T(8,128)}, f32[1,128,768]{2,1,0:T(8,128)}, u32[]{:S(2)}, u32[]{:S(2)}) collective-permute-start(f32[1,128,768]{2,1,0:T(8,128)} %get-tuple-element.167), channel_id=1, source_target_pairs={{0,1},{1,2},{2,3},{3,4},{4,5},{5,6},{6,7},{7,8},{8,9},{9,10},{10,1... | collective-permute-start | bytes 1179656 | tf_op jit(solution)/shard_map/ppermute | solution.py:45
  438.7 12.0 %collective-permute-start.4 = (f32[1,128,768]{2,1,0:T(8,128)}, f32[1,128,768]{2,1,0:T(8,128)}, u32[]{:S(2)}, u32[]{:S(2)}) collective-permute-start(f32[1,128,768]{2,1,0:T(8,128)} %get-tuple-element.168), channel_id=1, source_target_pairs={{0,32},{32,64},{64,96},{96,128},{128,160},{160,192},{192,224},{224... | collective-permute-start | bytes 1179656 | tf_op jit(solution)/shard_map/ppermute | solution.py:45
  442.4 17.1 %collective-permute-start.5 = (f32[1,128,768]{2,1,0:T(8,128)}, f32[1,128,768]{2,1,0:T(8,128)}, u32[]{:S(2)}, u32[]{:S(2)}) collective-permute-start(f32[1,128,768]{2,1,0:T(8,128)} %get-tuple-element.165), channel_id=1, source_target_pairs={{32,0},{64,32},{96,64},{128,96},{160,128},{192,160},{224,192},{256... | collective-permute-start | bytes 1179656 | tf_op jit(solution)/shard_map/ppermute | solution.py:45
  (5 other events, 6.1 us)
Sparse Core Ops, SparseCore 0:
  200.0 128.7 reduce-scatter.1
